TPU v7x, 256 devices: a whole 4x4x8 slice. The times are simulated.
256 devices in a mesh: tm: 8 (over z), lat: 32 (over y, x, core).
Axes of the slice: x: 4, y: 4, z: 8, core: 2. Of those that a mesh axis runs over, the one named last changes fastest.
Arguments:
- wind_east: bfloat16 [960, 256, 1440], P('tm', 'lat'), may hold values from -40 to 40
- wind_north: bfloat16 [960, 256, 1440], P('tm', 'lat'), may hold values from -40 to 40
- snap_counts: int32 [8], P('tm'), may hold values from 1 to 120, 320 in all
- snap_ids: int32 [960], P('tm'), may hold values from 0 to 8759
Outputs:
- basis: bfloat16 [32, 256, 1440], P(None, 'lat')
- coeffs: float32 [32, 960], P(None, 'tm')
Inputs may be any that keep to these rules, and one draw needn't show every extreme that they name: `snap_counts`: entry b counts the used slots of the b-th block of 120 slots, which are that block's first ones; the entries sum to 320 and one of them equals 120.
All inputs are finite; a program needn't handle non-finite values.
Results may differ from a plain program's by a relative error of at most 0.0072.
Values may be sent and summed in bfloat16 or wider, within the bound.
A program may use at most 64 MiB of HBM per device.

v0:
```python
import jax
import jax.numpy as jnp
from jax import lax
from jax.sharding import PartitionSpec as P

RANK = 32


def with_halo(cells, sides, width):
    for axis, dim in sides:
        count = lax.axis_size(axis)
        ends = count - 1
        head = lax.slice_in_dim(cells, 0, width, axis=dim)
        tail = lax.slice_in_dim(cells, cells.shape[dim] - width, cells.shape[dim], axis=dim)
        cells = jnp.concatenate(
            [
                lax.ppermute(tail, axis, [(i, (i + 1) % count) for i in range(ends)]),
                cells,
                lax.ppermute(head, axis, [((i + 1) % count, i) for i in range(ends)]),
            ],
            axis=dim,
        )
    return cells


def latitude_cosine(first_row, row_count, total_rows):
    row_index = first_row + jnp.arange(row_count, dtype=jnp.int32)
    return jnp.cos((total_rows // 2 - row_index).astype(jnp.float32) * (jnp.pi / 720.0))


def sign_table(snap_ids, rank_count):
    column = jnp.arange(rank_count, dtype=jnp.int32)
    mixed = snap_ids[:, None] * 1103515245 + column[None, :] * 40503 + 12345
    mixed = jnp.bitwise_xor(mixed, jnp.right_shift(mixed, 13))
    mixed = mixed * 1664525 + 1013904223
    mixed = jnp.bitwise_xor(mixed, jnp.right_shift(mixed, 16))
    flipped = jnp.bitwise_and(jnp.right_shift(mixed, 7), 1)
    return (1 - 2 * flipped).astype(jnp.bfloat16)


def metric_vorticity(padded_east, wind_north, padded_cosine, valid):
    scaled = padded_east.astype(jnp.float32) * padded_cosine[None, :, None]
    north_side = scaled[:, :-2]
    south_side = scaled[:, 2:]
    meridional = wind_north.astype(jnp.float32)
    zonal_diff = jnp.roll(meridional, -1, axis=2) - jnp.roll(meridional, 1, axis=2)
    weight = 0.5 / jnp.sqrt(padded_cosine[1:-1])
    field = (zonal_diff - north_side + south_side) * weight[None, :, None] * valid[:, None, None]
    return field.astype(jnp.bfloat16)


def local_gram(sketch, cell_total):
    return (
        lax.dot_general(
            sketch,
            sketch,
            (((1,), (1,)), ((), ())),
            precision=lax.Precision.HIGHEST,
            preferred_element_type=jnp.float32,
        )
        / cell_total
    )


def orthonormal(gram_sum, sketch):
    factor = jnp.linalg.cholesky(gram_sum)
    inverse = lax.linalg.triangular_solve(
        factor, jnp.eye(gram_sum.shape[0], dtype=jnp.float32), left_side=True, lower=True
    )
    return jnp.dot(
        inverse, sketch, precision=lax.Precision.HIGHEST, preferred_element_type=jnp.float32
    ).astype(jnp.bfloat16)


def local(wind_east, wind_north, snap_counts, snap_ids):
    snap_slots, band_rows, lon_count = wind_east.shape
    band_count = lax.axis_size("lat")
    first_row = lax.axis_index("lat") * band_rows - 1
    padded_cosine = latitude_cosine(first_row, band_rows + 2, band_rows * band_count)
    valid = (jnp.arange(snap_slots, dtype=jnp.int32) < snap_counts[0]).astype(jnp.float32)
    padded_east = with_halo(wind_east, (("lat", 1),), 1)
    field = metric_vorticity(padded_east, wind_north, padded_cosine, valid).reshape(
        snap_slots, band_rows * lon_count
    )
    signs_matrix = sign_table(snap_ids, RANK)
    sketch = jnp.dot(signs_matrix.T, field, preferred_element_type=jnp.float32)
    cell_total = band_rows * band_count * lon_count
    sketch = lax.psum(sketch, "tm")
    gram_sum = lax.psum(local_gram(sketch, cell_total), "lat")
    basis_flat = orthonormal(gram_sum, sketch)
    projected = (
        lax.dot_general(
            basis_flat, field, (((1,), (1,)), ((), ())), preferred_element_type=jnp.float32
        )
        / cell_total
    )
    coeffs = lax.psum(projected, "lat")
    return (basis_flat.reshape(basis_flat.shape[0], band_rows, lon_count), coeffs)


def solution(mesh):
    in_specs = (P("tm", "lat", None), P("tm", "lat", None), P("tm"), P("tm"))
    out_specs = (P(None, "lat", None), P(None, "tm"))
    return jax.shard_map(local, mesh=mesh, in_specs=in_specs, out_specs=out_specs, check_vma=False)
```

profile of v0, /device:TPU:32, one launch (start us, length us, event | category | flops | bytes accessed | tf_op | source)
XLA Modules:
  0.0 398.7 jit_solution(5653867448975015679)
XLA Ops:
  7.2 0.0 copy-start
  7.2 0.0 all-reduce.2.cloned.1.call-start
  7.2 4.0 %fusion.36 = (bf16[120,1,1440]{2,1,0:T(2,128)(2,1)S(1)}, bf16[120,1,1440]{2,1,0:T(2,128)(2,1)S(1)}) fusion(bf16[120,8,1440]{2,1,0:T(8,128)(2,1)} %param.4), kind=kLoop, calls=%fused_computation.55 | loop fusion | bytes 1382400 | tf_op jit(solution)/shard_map/slice | solution.py:14
  11.2 0.8 copy.21
  12.0 2.5 collective-permute-start
  14.5 0.8 copy.22
  15.3 1.3 collective-permute-start.1
  16.7 0.0 copy-done
  16.7 0.0 copy-start.3
  16.7 6.0 %fusion.35 = (f32[120,8,1439]{2,1,0:T(8,128)}, f32[120,8,1439]{2,1,0:T(8,128)}) fusion(bf16[120,8,1440]{2,1,0:T(8,128)(2,1)S(1)} %copy-done), kind=kLoop, calls=%fused_computation.54 | loop fusion | bytes 22103040 | tf_op jit(solution)/shard_map/jit(_roll_static)/slice | solution.py:46
  22.7 0.0 copy-start.1
  22.7 0.1 rsqrt_multiply_fusion
  23.6 0.0 copy-done.3
  23.6 0.9 fusion.34
  24.5 0.0 collective-permute-done
  24.5 1.6 copy.16
  26.0 0.0 collective-permute-done.1
  26.1 0.0 slice-start
  26.1 1.7 copy.17
  27.8 0.0 copy-done.1
  27.8 0.0 slice-start.1
  27.8 0.0 copy-start.2
  27.8 3.5 convert_multiply_fusion
  31.3 0.0 slice-done
  31.3 0.0 slice-done.1
  31.3 0.0 copy-done.2
  31.4 6.7 %fusion.2 = bf16[120,8,1440]{2,1,0:T(8,128)(2,1)} fusion(f32[120,10,1440]{2,1,0:T(8,128)S(1)} %convert_multiply_fusion, f32[120,8,1]{2,1,0:T(8,128)S(1)} %copy-done.2, f32[120,8,1439]{2,1,0:T(8,128)} %get-tuple-element.5, f32[120,8,1439]{2,1,0:T(8,128)S(1)} %bitcast.19, f32[120,8,1]{2,1,0:T(8,128)S(1)} %get-tuple-element.2, f32[120]{0:T(128)S(1)} %compare_convert_fusion, ...), kind=kLoop, calls=%fused_computation.5 | loop fusion | flops 11059200 | bytes 24883712 | tf_op jit(solution)/shard_map/convert_element_type | solution.py:49
  38.0 5.6 %reshape.40 = bf16[120,11520]{1,0:T(8,128)(2,1)S(1)} reshape(bf16[120,8,1440]{2,1,0:T(8,128)(2,1)} %fusion.2) | data formatting | bytes 5529600 | tf_op jit(solution)/shard_map/reshape | solution.py:82
  43.7 1.7 fusion.14
  45.4 0.0 all-reduce.2.cloned.1.call-update
  45.4 82.4 %all-reduce.2.cloned.1.call-done = f32[32,11520]{1,0:T(8,128)} async-done(((f32[32,11520]{1,0:T(8,128)}), f32[32,11520]{1,0:T(8,128)}) %all-reduce.2.cloned.1.call-update) | async-done | bytes 1474576 | tf_op jit(solution)/shard_map/psum | solution.py:88
  127.8 3.2 convolution_multiply_fusion.1
  131.0 124.3 %psum.22 = f32[32,32]{0,1:T(8,128)S(1)} all-reduce(f32[32,32]{0,1:T(8,128)S(1)} %convolution_multiply_fusion.1), channel_id=1, replica_groups=mesh['tm'=8,'lat'=32] {'lat'}, use_global_device_ids=true, to_apply=%region_1.2 | all-reduce | flops 1024 | bytes 8192 | tf_op jit(solution)/shard_map/psum | solution.py:89
  255.3 0.1 copy.19
  255.4 2.9 cholesky.17
  258.3 0.6 compare_reduce_fusion
  259.0 0.7 fusion.3
  259.6 2.4 custom-call.6
  262.1 0.2 fusion.11
  262.3 2.7 convolution_convert_fusion
  265.0 0.9 convolution_multiply_fusion
  266.0 2.1 reshape.41
  268.1 123.8 %psum.23 = f32[32,120]{1,0:T(8,128)} all-reduce(f32[32,120]{1,0:T(8,128)S(1)} %convolution_multiply_fusion), channel_id=1, replica_groups=mesh['tm'=8,'lat'=32] {'lat'}, use_global_device_ids=true, to_apply=%region_4.5 | all-reduce | flops 3840 | bytes 30720 | tf_op jit(solution)/shard_map/psum | solution.py:97
  (7 shorter events, 0.1 us)
Async XLA Ops:
  7.2 9.5 %copy-start = (bf16[120,8,1440]{2,1,0:T(8,128)(2,1)S(1)}, bf16[120,8,1440]{2,1,0:T(8,128)(2,1)}, u32[]{:S(2)}) copy-start(bf16[120,8,1440]{2,1,0:T(8,128)(2,1)} %param.5) | copy-start | bytes 8294404
  7.2 120.6 %all-reduce.2.cloned.1.call-start = ((), (), s32[]{:S(2)}) async-start(), calls=%async_computation | async-start | bytes 2949120 | tf_op jit(solution)/shard_map/psum | solution.py:88
  12.0 12.4 %collective-permute-start = (bf16[120,1,1440]{2,0,1:T(8,128)(2,1)}, bf16[120,1,1440]{2,0,1:T(8,128)(2,1)}, u32[]{:S(2)}, u32[]{:S(2)}) collective-permute-start(bf16[120,1,1440]{2,0,1:T(8,128)(2,1)} %copy.21), channel_id=1, source_target_pairs={{0,1},{1,2},{2,3},{3,4},{4,5},{5,6},{6,7},{7,8},{8,9},{9,10},{10,1... | collective-permute-start | bytes 1036808 | tf_op jit(solution)/shard_map/ppermute | solution.py:17
  15.3 10.7 %collective-permute-start.1 = (bf16[120,1,1440]{2,0,1:T(8,128)(2,1)}, bf16[120,1,1440]{2,0,1:T(8,128)(2,1)}, u32[]{:S(2)}, u32[]{:S(2)}) collective-permute-start(bf16[120,1,1440]{2,0,1:T(8,128)(2,1)} %copy.22), channel_id=1, source_target_pairs={{1,0},{2,1},{3,2},{4,3},{5,4},{6,5},{7,6},{8,7},{9,8},{10,9},{11,1... | collective-permute-start | bytes 1036808 | tf_op jit(solution)/shard_map/ppermute | solution.py:19
  16.7 6.9 %copy-start.3 = (s32[120]{0:T(128)S(1)}, s32[120]{0:T(128)}, u32[]{:S(2)}) copy-start(s32[120]{0:T(128)} %param.7) | copy-start | bytes 1444
  22.7 5.1 %copy-start.1 = (bf16[120,8,1440]{2,1,0:T(8,128)(2,1)S(1)}, bf16[120,8,1440]{2,1,0:T(8,128)(2,1)}, u32[]{:S(2)}) copy-start(bf16[120,8,1440]{2,1,0:T(8,128)(2,1)} %param.4) | copy-start | bytes 8294404
  26.1 5.3 %slice-start = ((s8[5898240]{0:T(1024)(128)(4,1)}), s8[4194304]{0:T(1024)(128)(4,1)S(1)}, s32[]{:S(2)}) async-start(s8[5898240]{0:T(1024)(128)(4,1)} %bitcast.18), calls=%async_computation.1 | async-start | bytes 8388608
  27.8 3.5 slice-start.1
  27.8 3.5 copy-start.2
Sparse Core Ops, SparseCore 0:
  45.5 82.2 all-reduce.1
where the time goes:
time: 399 us
  blocking collectives  248 us (62%)
  waiting for transfers between devices  82.5 us (21%)
  local copies, waits for them, and re-layouts  23.6 us (6%)
  other arithmetic  17 us (4%)
  between operations  15 us (4%)
  matrix products  8.73 us (2%)
    psum x1, blocking collectives, local(): gram_sum = lax.psum(local_gram(sketch, cell_total), 'lat')  124 us
    psum x1, blocking collectives, local(): coeffs = lax.psum(projected, 'lat')  124 us
    psum x1, waiting for transfers between devices, local(): sketch = lax.psum(sketch, 'tm')  82.4 us
  transfers between devices with their start and end apart: 3, of which 1 were waited for; matrix products, arithmetic and copies ran while one was open for 2% of the time, Pallas kernels for 0%

commit v1 on v0

--- a/solution.py
+++ b/solution.py
@@ -94,7 +94,7 @@
         )
         / cell_total
     )
-    coeffs = lax.psum(projected, "lat")
+    coeffs = jnp.sum(lax.all_gather(projected, "lat"), axis=0)
     return (basis_flat.reshape(basis_flat.shape[0], band_rows, lon_count), coeffs)
 
 

time: 399 us -> 300 us (0.75)
  blocking collectives: 248 us -> 146 us
    psum x1 -> x0, blocking collectives: 124 us -> none  [local(): coeffs = lax.psum(projected, 'lat')]
    all_gather x0 -> x1, blocking collectives: none -> 21.8 us  [local(): coeffs = jnp.sum(lax.all_gather(projected, 'lat'), axis=0)]
  transfers between devices with their start and end apart: 3 -> 3, of which waited for: 1 -> 1; matrix products, arithmetic and copies ran while one was open for 2% -> 3% of each run, Pallas kernels for 0% -> 0%
where the time goes in v1:
time: 300 us; the launch traced here: 297 us
  blocking collectives  146 us (49%)
  waiting for transfers between devices  82.5 us (28%)
  local copies, waits for them, and re-layouts  23.6 us (8%)
  other arithmetic  17.6 us (6%)
  between operations  15 us (5%)
  matrix products  8.73 us (3%)
  starting transfers between devices  3.82 us (1%)
    psum x1, blocking collectives, local(): gram_sum = lax.psum(local_gram(sketch, cell_total), 'lat')  124 us
    psum x1, waiting for transfers between devices, local(): sketch = lax.psum(sketch, 'tm')  82.4 us
    all_gather x1, blocking collectives, local(): coeffs = jnp.sum(lax.all_gather(projected, 'lat'), axis=0)  21.8 us
    slice x2, local copies, waits for them, and re-layouts, metric_vorticity(): jnp.roll(meridional, 1, axis=2)  6.85 us
    convert_element_type x1, other arithmetic, metric_vorticity(): return field.astype(jnp.bfloat16)  6.66 us
  transfers between devices with their start and end apart: 3, of which 1 were waited for; matrix products, arithmetic and copies ran while one was open for 3% of the time, Pallas kernels for 0%

profile of v1, /device:TPU:32, one launch (start us, length us, event | category | flops | bytes accessed | tf_op | source)
XLA Modules:
  0.0 297.4 jit_solution(4075411096195741940)
XLA Ops:
  7.2 0.0 copy-start
  7.2 0.0 all-reduce.2.cloned.1.call-start
  7.2 4.0 %fusion.36 = (bf16[120,1,1440]{2,1,0:T(2,128)(2,1)S(1)}, bf16[120,1,1440]{2,1,0:T(2,128)(2,1)S(1)}) fusion(bf16[120,8,1440]{2,1,0:T(8,128)(2,1)} %param.4), kind=kLoop, calls=%fused_computation.55 | loop fusion | bytes 1382400 | tf_op jit(solution)/shard_map/slice | solution.py:14
  11.2 0.8 copy.21
  12.0 2.5 collective-permute-start
  14.5 0.8 copy.22
  15.3 1.3 collective-permute-start.1
  16.7 0.0 copy-done
  16.7 0.0 copy-start.3
  16.7 6.0 %fusion.35 = (f32[120,8,1439]{2,1,0:T(8,128)}, f32[120,8,1439]{2,1,0:T(8,128)}) fusion(bf16[120,8,1440]{2,1,0:T(8,128)(2,1)S(1)} %copy-done), kind=kLoop, calls=%fused_computation.54 | loop fusion | bytes 22103040 | tf_op jit(solution)/shard_map/jit(_roll_static)/slice | solution.py:46
  22.7 0.0 copy-start.1
  22.7 0.1 rsqrt_multiply_fusion
  23.6 0.0 copy-done.3
  23.6 0.9 fusion.34
  24.5 0.0 collective-permute-done
  24.5 1.6 copy.16
  26.0 0.0 collective-permute-done.1
  26.1 0.0 slice-start
  26.1 1.7 copy.17
  27.8 0.0 copy-done.1
  27.8 0.0 slice-start.1
  27.8 0.0 copy-start.2
  27.8 3.5 %convert_multiply_fusion = f32[120,10,1440]{2,1,0:T(8,128)S(1)} fusion(bf16[120,1,1440]{2,1,0:T(2,128)(2,1)S(1)} %copy.17, bf16[120,8,1440]{2,1,0:T(8,128)(2,1)S(1)} %copy-done.1, bf16[120,1,1440]{2,1,0:T(2,128)(2,1)S(1)} %copy.16, f32[10]{0:T(128)S(1)} %multiply_cosine_fusion), kind=kLoop, calls=%fused_computation.1 | loop fusion | flops 12096000 | bytes 10368040 | tf_op jit(solution)/shard_map/mul | solution.py:42
  31.3 0.0 slice-done
  31.3 0.0 slice-done.1
  31.3 0.0 copy-done.2
  31.4 6.7 %fusion.2 = bf16[120,8,1440]{2,1,0:T(8,128)(2,1)} fusion(f32[120,10,1440]{2,1,0:T(8,128)S(1)} %convert_multiply_fusion, f32[120,8,1]{2,1,0:T(8,128)S(1)} %copy-done.2, f32[120,8,1439]{2,1,0:T(8,128)} %get-tuple-element.5, f32[120,8,1439]{2,1,0:T(8,128)S(1)} %bitcast.20, f32[120,8,1]{2,1,0:T(8,128)S(1)} %get-tuple-element.2, f32[120]{0:T(128)S(1)} %compare_convert_fusion, ...), kind=kLoop, calls=%fused_computation.5 | loop fusion | flops 11059200 | bytes 24883712 | tf_op jit(solution)/shard_map/convert_element_type | solution.py:49
  38.0 5.6 %reshape.40 = bf16[120,11520]{1,0:T(8,128)(2,1)S(1)} reshape(bf16[120,8,1440]{2,1,0:T(8,128)(2,1)} %fusion.2) | data formatting | bytes 5529600 | tf_op jit(solution)/shard_map/reshape | solution.py:82
  43.7 1.7 fusion.14
  45.4 0.0 all-reduce.2.cloned.1.call-update
  45.4 82.4 %all-reduce.2.cloned.1.call-done = f32[32,11520]{1,0:T(8,128)} async-done(((f32[32,11520]{1,0:T(8,128)}), f32[32,11520]{1,0:T(8,128)}) %all-reduce.2.cloned.1.call-update) | async-done | bytes 1474576 | tf_op jit(solution)/shard_map/psum | solution.py:88
  127.8 3.2 %convolution_multiply_fusion.1 = f32[32,32]{0,1:T(8,128)S(1)} fusion(f32[32,11520]{1,0:T(8,128)} %all-reduce.2.cloned.1.call-done), kind=kOutput, calls=%fused_computation.9 | convolution fusion | flops 141558784 | bytes 1478656 | tf_op jit(solution)/shard_map/dot_general | solution.py:54
  131.0 124.3 %psum.15 = f32[32,32]{0,1:T(8,128)S(1)} all-reduce(f32[32,32]{0,1:T(8,128)S(1)} %convolution_multiply_fusion.1), channel_id=1, replica_groups=mesh['tm'=8,'lat'=32] {'lat'}, use_global_device_ids=true, to_apply=%region_1.2 | all-reduce | flops 1024 | bytes 8192 | tf_op jit(solution)/shard_map/psum | solution.py:89
  255.3 0.1 copy.19
  255.4 2.9 cholesky.17
  258.3 0.6 compare_reduce_fusion
  259.0 0.7 fusion.3
  259.6 2.4 custom-call.6
  262.1 0.2 fusion.11
  262.3 2.7 convolution_convert_fusion
  265.0 0.9 convolution_multiply_fusion
  266.0 2.1 reshape.41
  268.1 21.8 %all-gather = f32[1024,120]{1,0:T(8,128)S(1)} all-gather(f32[32,120]{1,0:T(8,128)S(1)} %convolution_multiply_fusion), channel_id=2, replica_groups=mesh['tm'=8,'lat'=32] {'lat'}, dimensions={0}, use_global_device_ids=true | all-gather | bytes 506880 | tf_op jit(solution)/shard_map/all_gather | solution.py:97
  289.9 0.7 reduce_sum.9
  (7 shorter events, 0.1 us)
Async XLA Ops:
  7.2 9.5 %copy-start = (bf16[120,8,1440]{2,1,0:T(8,128)(2,1)S(1)}, bf16[120,8,1440]{2,1,0:T(8,128)(2,1)}, u32[]{:S(2)}) copy-start(bf16[120,8,1440]{2,1,0:T(8,128)(2,1)} %param.5) | copy-start | bytes 8294404
  7.2 120.6 %all-reduce.2.cloned.1.call-start = ((), (), s32[]{:S(2)}) async-start(), calls=%async_computation | async-start | bytes 2949120 | tf_op jit(solution)/shard_map/psum | solution.py:88
  12.0 12.4 %collective-permute-start = (bf16[120,1,1440]{2,0,1:T(8,128)(2,1)}, bf16[120,1,1440]{2,0,1:T(8,128)(2,1)}, u32[]{:S(2)}, u32[]{:S(2)}) collective-permute-start(bf16[120,1,1440]{2,0,1:T(8,128)(2,1)} %copy.21), channel_id=1, source_target_pairs={{0,1},{1,2},{2,3},{3,4},{4,5},{5,6},{6,7},{7,8},{8,9},{9,10},{10,1... | collective-permute-start | bytes 1036808 | tf_op jit(solution)/shard_map/ppermute | solution.py:17
  15.3 10.7 %collective-permute-start.1 = (bf16[120,1,1440]{2,0,1:T(8,128)(2,1)}, bf16[120,1,1440]{2,0,1:T(8,128)(2,1)}, u32[]{:S(2)}, u32[]{:S(2)}) collective-permute-start(bf16[120,1,1440]{2,0,1:T(8,128)(2,1)} %copy.22), channel_id=1, source_target_pairs={{1,0},{2,1},{3,2},{4,3},{5,4},{6,5},{7,6},{8,7},{9,8},{10,9},{11,1... | collective-permute-start | bytes 1036808 | tf_op jit(solution)/shard_map/ppermute | solution.py:19
  16.7 6.9 %copy-start.3 = (s32[120]{0:T(128)S(1)}, s32[120]{0:T(128)}, u32[]{:S(2)}) copy-start(s32[120]{0:T(128)} %param.7) | copy-start | bytes 1444
  22.7 5.1 %copy-start.1 = (bf16[120,8,1440]{2,1,0:T(8,128)(2,1)S(1)}, bf16[120,8,1440]{2,1,0:T(8,128)(2,1)}, u32[]{:S(2)}) copy-start(bf16[120,8,1440]{2,1,0:T(8,128)(2,1)} %param.4) | copy-start | bytes 8294404
  26.1 5.3 %slice-start = ((s8[5898240]{0:T(1024)(128)(4,1)}), s8[4194304]{0:T(1024)(128)(4,1)S(1)}, s32[]{:S(2)}) async-start(s8[5898240]{0:T(1024)(128)(4,1)} %bitcast.19), calls=%async_computation.1 | async-start | bytes 8388608
  27.8 3.5 %slice-start.1 = ((s8[5898240]{0:T(1024)(128)(4,1)}), s8[1703936]{0:T(1024)(128)(4,1)S(1)}, s32[]{:S(2)}) async-start(s8[5898240]{0:T(1024)(128)(4,1)} %bitcast.19), calls=%async_computation.2 | async-start | bytes 3407872
  27.8 3.5 %copy-start.2 = (f32[120,8,1]{2,1,0:T(8,128)S(1)}, f32[120,8,1]{2,1,0:T(8,128)}, u32[]{:S(2)}) copy-start(f32[120,8,1]{2,1,0:T(8,128)} %get-tuple-element.3) | copy-start | bytes 11524
Sparse Core Ops, SparseCore 0:
  45.5 82.2 all-reduce.1
